TPU v7x, 32 devices: a whole 2x2x4 slice. The times are simulated.
32 devices in a mesh: groups: 2 (over x), dp: 8 (over z, y), mp: 2 (over core).
Axes of the slice: x: 2, y: 2, z: 4, core: 2. Of those that a mesh axis runs over, the one named last changes fastest.
Arguments:
- residual: bfloat16 [48, 128, 8192], P(('groups', 'dp'), None, 'mp'), parts along dimension 0
- lengths: int32 [48], P(('groups', 'dp')), parts along dimension 0, may hold values from 32 to 128
- labels: int32 [48], P(('groups', 'dp')), parts along dimension 0, may hold values from 0 to 1, as said below
- earlier_means: float32 [16, 79, 2, 8192], P(('groups', 'dp'), None, None, 'mp'), parts along dimension 0
- chosen: int32 [2], P('groups'), parts along dimension 0, may hold values from 0 to 79
- norm_gain: float32 [8192], P('mp'), may hold values from 0.1 to 1.9
- key_weight: bfloat16 [2, 4096, 1024], P('mp', 'dp'), may hold values from -0.0625 to 0.0625
- value_weight: bfloat16 [2, 4096, 1024], P('mp', 'dp'), may hold values from -0.0625 to 0.0625
- out_proj: bfloat16 [2, 8192, 8192], P('groups', 'mp', 'dp'), parts along dimension 0
Outputs:
- directions: float32 [160, 8192], P('groups', 'mp'), parts along dimension 0
- key_cache: bfloat16 [48, 128, 1024], P(('groups', 'dp'), None, 'mp'), parts along dimension 0
- value_cache: bfloat16 [48, 128, 1024], P(('groups', 'dp'), None, 'mp'), parts along dimension 0
- ortho_proj: bfloat16 [2, 8192, 8192], P('groups', 'mp', 'dp'), parts along dimension 0
There are 2 independent parts, one for each index of `groups`. A program takes and returns all parts, laid end to end along the dimension named above; an argument that names none is the same for every part. Nothing has to cross between parts.
Inputs may be any that keep to these rules, and one draw needn't show every extreme that they name: Every slab of 3 consecutive prompts holds both labels.
All inputs are finite; a program needn't handle non-finite values.
Results may differ from a plain program's by a relative error of at most 0.0051.
Values may be sent and summed in bfloat16 or wider, within the bound.
A program may use at most 384 MiB of HBM per device.

v0:
```python
import math
import jax
import jax.numpy as jnp
from jax import lax
from jax.sharding import PartitionSpec as P


def joined(value, axis, join):
    pieces = jax.tree.map(lambda part: lax.all_gather(part, axis), value)
    head = jax.tree.map(lambda part: part[0], pieces)
    tail = jax.tree.map(lambda part: part[1:], pieces)
    total, _ = lax.scan(lambda total, share: (join(total, share), None), head, tail)
    return total


def shards(
    residual, lengths, labels, earlier_means, chosen, norm_gain, key_weight, value_weight, out_proj
):
    highest = lax.Precision.HIGHEST
    prompts, length, half_width = residual.shape
    model_width = half_width * lax.axis_size("mp")
    positions = jnp.arange(length, dtype=jnp.int32)
    valid_mask = (positions[None, :] < lengths[:, None]).astype(jnp.bfloat16)
    masked_sums = jnp.einsum("pt,ptd->pd", valid_mask, residual, preferred_element_type=jnp.float32)
    prompt_mean = masked_sums / lengths.astype(jnp.float32)[:, None]
    onehot = (labels[:, None] == jnp.arange(2, dtype=jnp.int32)[None, :]).astype(jnp.float32)
    counts = jnp.sum(onehot, axis=0)
    current = jnp.dot(onehot.T, prompt_mean, precision=highest) / counts[:, None]
    layer_means = jnp.concatenate([earlier_means[0], current[None]], axis=0)

    def combine(left_pair, right_pair):
        joint_count = left_pair[0] + right_pair[0]
        blended = (
            left_pair[0][None, :, None] * left_pair[1]
            + right_pair[0][None, :, None] * right_pair[1]
        )
        return (joint_count, blended / joint_count[None, :, None])

    merged_counts, merged = joined((counts, layer_means), "dp", combine)
    difference = merged[:, 1] - merged[:, 0]
    square_sums = lax.psum(jnp.sum(difference * difference, axis=1), "mp")
    mean_dir = square_sums / model_width
    inverse_rms = lax.rsqrt(mean_dir + 1e-06)
    directions = difference * inverse_rms[:, None]
    chosen_layer = chosen[0]
    refusal_dir = lax.dynamic_index_in_dim(directions, chosen_layer, 0, keepdims=False) / math.sqrt(
        model_width
    )
    token_rows = residual.reshape(prompts * length, half_width)
    row_values = token_rows.astype(jnp.float32)
    projection_local = jnp.dot(row_values, refusal_dir, precision=highest)
    column_local = jnp.einsum(
        "r,ori->oi", refusal_dir, out_proj.astype(jnp.float32), precision=highest
    )
    projection, column_proj = lax.psum((projection_local, column_local), "mp")
    ablated = row_values - projection[:, None] * refusal_dir[None, :]
    mean_square = lax.psum(jnp.sum(ablated * ablated, axis=1), "mp") / model_width
    normed = (ablated * lax.rsqrt(mean_square + 1e-05)[:, None] * norm_gain[None, :]).astype(
        jnp.bfloat16
    )
    key_sum = jnp.dot(
        normed,
        lax.all_gather(key_weight, "dp", axis=1, tiled=True)[0],
        preferred_element_type=jnp.float32,
    )
    value_sum = jnp.dot(
        normed,
        lax.all_gather(value_weight, "dp", axis=1, tiled=True)[0],
        preferred_element_type=jnp.float32,
    )
    key_sums, value_sums = (
        lax.psum_scatter(key_sum, "mp", scatter_dimension=1, tiled=True),
        lax.psum_scatter(value_sum, "mp", scatter_dimension=1, tiled=True),
    )
    key_cache = key_sums.astype(jnp.bfloat16).reshape(prompts, length, key_sums.shape[1])
    value_cache = value_sums.astype(jnp.bfloat16).reshape(prompts, length, value_sums.shape[1])
    ortho_proj = (
        out_proj.astype(jnp.float32) - refusal_dir[None, :, None] * column_proj[:, None, :]
    ).astype(jnp.bfloat16)
    return (directions, key_cache, value_cache, ortho_proj)


def solution(mesh):
    return jax.shard_map(
        shards,
        mesh=mesh,
        in_specs=(
            P(("groups", "dp"), None, "mp"),
            P(("groups", "dp")),
            P(("groups", "dp")),
            P(("groups", "dp"), None, None, "mp"),
            P("groups"),
            P("mp"),
            P("mp", "dp", None),
            P("mp", "dp", None),
            P("groups", "mp", "dp"),
        ),
        out_specs=(
            P("groups", "mp"),
            P(("groups", "dp"), None, "mp"),
            P(("groups", "dp"), None, "mp"),
            P("groups", "mp", "dp"),
        ),
        check_vma=False,
    )
```

profile of v0, /device:TPU:0, one launch (start us, length us, event | category | flops | bytes accessed | tf_op | source)
XLA Modules:
  0.0 703.0 jit_solution(7702679912213129711)
XLA Ops:
  12.2 2.8 pad_maximum_fusion
  17.5 48.1 %all-reduce = f32[16]{0:T(128)S(1)} all-reduce(f32[16]{0:T(128)S(1)} %dynamic-update-slice), channel_id=2, replica_groups=mesh['groups'=2,'dp'=8,'mp'=2] {'dp'}, use_global_device_ids=true, to_apply=%add | all-reduce | flops 16 | bytes 128
  66.4 353.8 %all-gather.10.cloned.1.call-done = f32[640,2,4096]{2,1,0:T(2,128)} async-done(((f32[80,2,4096]{2,1,0:T(2,128)}), f32[640,2,4096]{2,1,0:T(2,128)}) %all-gather.10.cloned.1.call-update) | async-done | bytes 20971536 | tf_op jit(solution)/shard_map/all_gather | solution.py:9
  420.3 13.6 %slice.29 = f32[560,2,4096]{2,1,0:T(2,128)} slice(f32[640,2,4096]{2,1,0:T(2,128)} %all-gather.10.cloned.1.call-done), slice={[80:640], [0:2], [0:4096]} | slice | bytes 36700160 | tf_op jit(solution)/shard_map/slice | solution.py:11
  435.6 32.7 %while.12 = (s32[]{:T(128)}, f32[2]{0:T(128)S(1)}, f32[80,2,4096]{2,1,0:T(2,128)S(1)}, f32[7,2]{1,0:T(8,128)S(1)}, f32[7,80,2,4096]{3,2,1,0:T(2,128)}, /*index=5*/s32[]{:T(128)}) while((s32[]{:T(128)}, f32[2]{0:T(128)S(1)}, f32[80,2,4096]{2,1,0:T(2,128)S(1)}, f32[7,2]{1,0:T(8,128)S(1)}, f32[7,80,2,4096]{3,2,1,0:T(2,128)}, ...), condition=%wide.region_2.3_spmd, body=%wide.region_1.2_spmd.sunk | while | flops 2621444 | bytes 7864469 | solution.py:12
  435.6 4.6 fusion.27
  440.3 4.6 fusion.27
  445.0 4.6 fusion.27
  449.6 4.6 fusion.27
  454.3 4.6 fusion.27
  459.0 4.6 fusion.27
  463.7 4.6 fusion.27
  471.6 2.6 psum.28
  477.5 2.6 convolution_reduce_fusion
  480.1 2.7 psum.29
  483.9 5.7 fusion.3
  489.6 2.5 all-reduce.1
  492.1 3.4 multiply_convert_fusion
  495.5 51.9 %all-gather.6.cloned.1.call-done = bf16[1,4096,1024]{2,1,0:T(8,128)(2,1)} async-done(((bf16[1,512,1024]{2,1,0:T(8,128)(2,1)}), bf16[1,4096,1024]{2,1,0:T(8,128)(2,1)}) %all-gather.6.cloned.1.call-update) | async-done | bytes 8388624 | tf_op jit(solution)/shard_map/all_gather | solution.py:63
  547.4 9.0 %fusion.7 = f32[384,1024]{1,0:T(8,128)} fusion(bf16[384,4096]{1,0:T(8,128)(2,1)} %bitcast.63, bf16[1,4096,1024]{2,1,0:T(8,128)(2,1)} %all-gather.6.cloned.1.call-done), kind=kOutput, calls=%fused_computation.10 | convolution fusion | flops 3221225472 | bytes 13107200 | tf_op jit(solution)/shard_map/dot_general | solution.py:61
  556.5 116.2 %all-gather.8.cloned.1.call-done = bf16[1,4096,1024]{2,1,0:T(8,128)(2,1)} async-done(((bf16[1,512,1024]{2,1,0:T(8,128)(2,1)}), bf16[1,4096,1024]{2,1,0:T(8,128)(2,1)}) %all-gather.8.cloned.1.call-update) | async-done | bytes 8388624 | tf_op jit(solution)/shard_map/all_gather | solution.py:68
  672.7 6.9 fusion.5
  679.6 7.9 %subtract_convert_fusion = bf16[1,4096,1024]{2,1,0:T(8,128)(2,1)} fusion(bf16[1,4096,1024]{2,1,0:T(8,128)(2,1)} %param.19, f32[1024]{0:T(1024)S(1)} %get-tuple-element.43, f32[4096]{0:T(1024)S(1)} %bitcast.68), kind=kLoop, calls=%fused_computation.5 | loop fusion | flops 16777216 | bytes 16797696 | tf_op jit(solution)/shard_map/convert_element_type | solution.py:79
  689.5 5.1 reduce-scatter.5.cloned.1.call-done
  (62 shorter events, 20.4 us)
Async XLA Ops:
  7.2 4.8 copy-start.6
  7.2 5.1 copy-start.3
  7.2 413.1 %all-gather.10.cloned.1.call-start = ((), (), s32[]{:S(2)}) async-start(), calls=%async_computation.6 | async-start | bytes 23592960 | tf_op jit(solution)/shard_map/all_gather | solution.py:9
  15.1 0.8 copy-start.7
  15.1 532.3 %all-gather.6.cloned.1.call-start = ((), (), s32[]{:S(2)}) async-start(), calls=%async_computation.2 | async-start | bytes 9437184 | tf_op jit(solution)/shard_map/all_gather | solution.py:63
  15.9 656.8 %all-gather.8.cloned.1.call-start = ((), (), s32[]{:S(2)}) async-start(), calls=%async_computation.4 | async-start | bytes 9437184 | tf_op jit(solution)/shard_map/all_gather | solution.py:68
  17.4 670.1 %reduce-scatter.3.cloned.1.call-start = ((), (), s32[]{:S(2)}) async-start(), calls=%async_computation.3 | async-start | bytes 2359296 | tf_op jit(solution)/shard_map/reduce_scatter | solution.py:72
  433.9 1.7 slice-start
  469.8 1.5 copy-start.1
  471.3 6.2 copy-start
  476.4 1.1 copy-start.4
  483.9 8.2 %copy-start.5 = (f32[4096]{0:T(1024)S(1)}, f32[4096]{0:T(1024)}, u32[]{:S(2)}) copy-start(f32[4096]{0:T(1024)} %param.16) | copy-start | bytes 49156
  547.4 125.3 %copy-start.2 = (bf16[3,128,4096]{2,1,0:T(8,128)(2,1)S(1)}, bf16[3,128,4096]{2,1,0:T(8,128)(2,1)}, u32[]{:S(2)}) copy-start(bf16[3,128,4096]{2,1,0:T(8,128)(2,1)} %multiply_convert_fusion) | copy-start | bytes 9437188
  556.4 138.1 %reduce-scatter.5.cloned.1.call-start = ((), (), s32[]{:S(2)}) async-start(), calls=%async_computation.5 | async-start | bytes 2359296 | tf_op jit(solution)/shard_map/reduce_scatter | solution.py:73
Sparse Core Ops, SparseCore 0:
  15.2 405.0 all-gather.9
  422.4 124.9 all-gather.5
  549.5 123.1 all-gather.7
  674.8 7.2 reduce-scatter.2
  684.2 10.2 reduce-scatter.4
where the time goes:
time: 704 us; the launch traced here: 703 us
  waiting for transfers between devices  528 us (75%)
  other arithmetic  56.4 us (8%)
  blocking collectives  55.9 us (8%)
  matrix products  26.9 us (4%)
  local copies, waits for them, and re-layouts  20.4 us (3%)
  between operations  15.2 us (2%)
    all_gather x1, waiting for transfers between devices, joined(): pieces = jax.tree.map(lambda part: lax.all_gather(part, axis), value)  354 us
    all_gather x1, waiting for transfers between devices, shards(): lax.all_gather(value_weight, 'dp', axis=1, tiled=True)[0]  116 us
    all_gather x1, waiting for transfers between devices, shards(): lax.all_gather(key_weight, 'dp', axis=1, tiled=True)[0]  51.9 us
    unnamed x1, blocking collectives  48.1 us
    div x7, other arithmetic, combine(): return (joint_count, blended / joint_count[None, :, None])  32.4 us
  transfers between devices with their start and end apart: 5, of which 4 were waited for; matrix products, arithmetic and copies ran while one was open for 13% of the time, Pallas kernels for 0%

commit v1 on v0

--- a/solution.py
+++ b/solution.py
@@ -58,11 +58,35 @@
     normed = (ablated * lax.rsqrt(mean_square + 1e-05)[:, None] * norm_gain[None, :]).astype(
         jnp.bfloat16
     )
-    key_sum = jnp.dot(
-        normed,
-        lax.all_gather(key_weight, "dp", axis=1, tiled=True)[0],
-        preferred_element_type=jnp.float32,
-    )
+
+    def put_skins(x_part):
+        which_axis = "dp"
+        block_next, all_values, w2 = (
+            lax.axis_size(which_axis),
+            lax.axis_index(which_axis),
+            x_part.shape[1],
+        )
+        items = tuple(((dev_j, (dev_j + 1) % block_next) for dev_j in range(block_next)))
+        views = tuple(((dev_j, (dev_j - 1) % block_next) for dev_j in range(block_next)))
+        wide_out = jnp.zeros((*x_part.shape[:1], block_next * w2, *x_part.shape[2:]), x_part.dtype)
+        wide_out = lax.dynamic_update_slice_in_dim(wide_out, x_part, all_values * w2, axis=1)
+        carry = formed = x_part
+        piece_out = block_next // 2
+        h = 1
+        while h < piece_out + 1:
+            carry = lax.ppermute(carry, which_axis, items)
+            wide_out = lax.dynamic_update_slice_in_dim(
+                wide_out, carry, (all_values - h) % block_next * w2, axis=1
+            )
+            if h < block_next - piece_out:
+                formed = lax.ppermute(formed, which_axis, perm=views)
+                wide_out = lax.dynamic_update_slice_in_dim(
+                    wide_out, formed, (all_values + h) % block_next * w2, axis=1
+                )
+            h += 1
+        return wide_out
+
+    key_sum = jnp.dot(normed, put_skins(key_weight)[0], preferred_element_type=jnp.float32)
     value_sum = jnp.dot(
         normed,
         lax.all_gather(value_weight, "dp", axis=1, tiled=True)[0],

time: 704 us -> 734 us (1.043)
  waiting for transfers between devices: 528 us -> 455 us
  blocking collectives: 55.9 us -> 113 us
  starting transfers between devices: 0.2 us -> 27.4 us
  local copies, waits for them, and re-layouts: 20.4 us -> 34.2 us
    ppermute x0 -> x7, waiting for transfers between devices: none -> 226 us  [the longest x3 120 us: put_skins(): formed = lax.ppermute(formed, which_axis, perm=views)]
    all_gather x1, waiting for transfers between devices: 354 us -> 181 us  [joined(): pieces = jax.tree.map(lambda part: lax.all_gather(part, axis), value)]
    all_gather x1, waiting for transfers between devices: 116 us -> 45.1 us  [shards(): lax.all_gather(value_weight, 'dp', axis=1, tiled=True)[0]]
    unnamed x1, blocking collectives: 48.1 us -> 106 us
    all_gather x1 -> x0, waiting for transfers between devices: 51.9 us -> none  [shards(): lax.all_gather(key_weight, 'dp', axis=1, tiled=True)[0]]
    ppermute x0 -> x7, starting transfers between devices: none -> 27.2 us  [the longest x3 19 us: put_skins(): formed = lax.ppermute(formed, which_axis, perm=views)]
    dynamic_update_slice x0 -> x8, local copies, waits for them, and re-layouts: none -> 10.8 us  [the longest x4 5.38 us: put_skins(): lax.dynamic_update_slice_in_dim(wide_out, carry, (all_values - h) % block...]
  transfers between devices with their start and end apart: 5 -> 11, of which waited for: 4 -> 6; matrix products, arithmetic and copies ran while one was open for 13% -> 14% of each run, Pallas kernels for 0% -> 0%
where the time goes in v1:
time: 734 us; the launch traced here: 733 us
  waiting for transfers between devices  455 us (62%)
  blocking collectives  113 us (15%)
  other arithmetic  59.4 us (8%)
  local copies, waits for them, and re-layouts  34.2 us (5%)
  matrix products  28.5 us (4%)
  starting transfers between devices  27.4 us (4%)
  between operations  15.4 us (2%)
    all_gather x1, waiting for transfers between devices, joined(): pieces = jax.tree.map(lambda part: lax.all_gather(part, axis), value)  181 us
    ppermute x3, waiting for transfers between devices, put_skins(): formed = lax.ppermute(formed, which_axis, perm=views)  120 us
    unnamed x1, blocking collectives  106 us
    ppermute x4, waiting for transfers between devices, put_skins(): carry = lax.ppermute(carry, which_axis, items)  105 us
    all_gather x1, waiting for transfers between devices, shards(): lax.all_gather(value_weight, 'dp', axis=1, tiled=True)[0]  45.1 us
    div x7, other arithmetic, combine(): return (joint_count, blended / joint_count[None, :, None])  32.4 us
    ppermute x3, starting transfers between devices, put_skins(): formed = lax.ppermute(formed, which_axis, perm=views)  19 us
  transfers between devices with their start and end apart: 11, of which 6 were waited for; matrix products, arithmetic and copies ran while one was open for 14% of the time, Pallas kernels for 0%

profile of v1, /device:TPU:0, one launch (start us, length us, event | category | flops | bytes accessed | tf_op | source)
XLA Modules:
  0.0 733.1 jit_solution(14823888851950455569)
XLA Ops:
  12.8 5.7 pad_maximum_fusion
  24.8 105.4 %collective-permute-done = bf16[1,512,1024]{2,1,0:T(8,128)(2,1)S(1)} collective-permute-done((bf16[1,512,1024]{2,1,0:T(8,128)(2,1)S(1)}, bf16[1,512,1024]{2,1,0:T(8,128)(2,1)S(1)}, u32[]{:S(2)}, u32[]{:S(2)}) %collective-permute-start) | collective-permute-done | bytes 1048608 | tf_op jit(solution)/shard_map/ppermute | solution.py:77
  132.6 37.6 %collective-permute-done.1 = bf16[1,512,1024]{2,1,0:T(8,128)(2,1)} collective-permute-done((bf16[1,512,1024]{2,1,0:T(8,128)(2,1)S(1)}, bf16[1,512,1024]{2,1,0:T(8,128)(2,1)}, u32[]{:S(2)}, u32[]{:S(2)}) %collective-permute-start.1) | collective-permute-done | bytes 1048608 | tf_op jit(solution)/shard_map/ppermute | solution.py:82
  170.2 15.9 %collective-permute-start.3 = (bf16[1,512,1024]{2,1,0:T(8,128)(2,1)}, bf16[1,512,1024]{2,1,0:T(8,128)(2,1)S(1)}, u32[]{:S(2)}, u32[]{:S(2)}) collective-permute-start(bf16[1,512,1024]{2,1,0:T(8,128)(2,1)} %collective-permute-done.1), channel_id=1, source_target_pairs={{0,14},{2,0},{4,2},{6,4},{8,6},{10,8},{12,10},{14,12},{1,15},{3,1}... | collective-permute-start | bytes 3145736 | tf_op jit(solution)/shard_map/ppermute | solution.py:82
  188.4 105.7 %all-reduce = f32[16]{0:T(128)S(1)} all-reduce(f32[16]{0:T(128)S(1)} %dynamic-update-slice), channel_id=2, replica_groups=mesh['groups'=2,'dp'=8,'mp'=2] {'dp'}, use_global_device_ids=true, to_apply=%add | all-reduce | flops 16 | bytes 128
  295.0 4.5 squeeze.50
  310.2 82.7 %collective-permute-done.5 = bf16[1,512,1024]{2,1,0:T(8,128)(2,1)S(1)} collective-permute-done((bf16[1,512,1024]{2,1,0:T(8,128)(2,1)S(1)}, bf16[1,512,1024]{2,1,0:T(8,128)(2,1)S(1)}, u32[]{:S(2)}, u32[]{:S(2)}) %collective-permute-start.5) | collective-permute-done | bytes 1048608 | tf_op jit(solution)/shard_map/ppermute | solution.py:82
  394.9 180.6 %all-gather.7.cloned.1.call-done = f32[640,2,4096]{2,1,0:T(2,128)} async-done(((f32[80,2,4096]{2,1,0:T(2,128)}), f32[640,2,4096]{2,1,0:T(2,128)}) %all-gather.7.cloned.1.call-update) | async-done | bytes 20971536 | tf_op jit(solution)/shard_map/all_gather | solution.py:9
  575.5 13.8 %slice.29 = f32[560,2,4096]{2,1,0:T(2,128)} slice(f32[640,2,4096]{2,1,0:T(2,128)} %all-gather.7.cloned.1.call-done), slice={[80:640], [0:2], [0:4096]} | slice | bytes 36700160 | tf_op jit(solution)/shard_map/slice | solution.py:11
  589.4 32.7 %while.12 = (s32[]{:T(128)}, f32[2]{0:T(128)S(1)}, f32[80,2,4096]{2,1,0:T(2,128)S(1)}, f32[7,2]{1,0:T(8,128)S(1)}, f32[7,80,2,4096]{3,2,1,0:T(2,128)}, /*index=5*/s32[]{:T(128)}) while((s32[]{:T(128)}, f32[2]{0:T(128)S(1)}, f32[80,2,4096]{2,1,0:T(2,128)S(1)}, f32[7,2]{1,0:T(8,128)S(1)}, f32[7,80,2,4096]{3,2,1,0:T(2,128)}, ...), condition=%wide.region_2.3_spmd, body=%wide.region_1.2_spmd.sunk | while | flops 2621444 | bytes 7864477 | solution.py:12
  589.4 4.6 fusion.31
  594.1 4.6 fusion.31
  598.8 4.6 fusion.31
  603.4 4.6 fusion.31
  608.1 4.6 fusion.31
  612.8 4.6 fusion.31
  617.4 4.6 fusion.31
  637.9 5.7 fusion.3
  646.1 8.0 %fusion.8 = f32[384,1024]{1,0:T(8,128)} fusion(bf16[4096,1024]{1,0:T(8,128)(2,1)} %bitcast_dynamic-update-slice_fusion, bf16[384,4096]{1,0:T(8,128)(2,1)S(1)} %bitcast.76, f32[4096]{0:T(1024)S(1)} %copy-done.6, f32[384]{0:T(512)S(1)} %get-tuple-element.47, f32[4096]{0:T(1024)S(1)} %bitcast.80, f32[384]{0:T(512)S(1)} %psum.29), kind=kOutput, calls=%fused_computation.16 | convolution fusion | flops 3230662656 | bytes 13143040 | tf_op jit(solution)/shard_map/dot_general | solution.py:89
  654.2 3.4 multiply_convert_fusion
  657.6 45.1 %all-gather.5.cloned.1.call-done = bf16[1,4096,1024]{2,1,0:T(8,128)(2,1)} async-done(((bf16[1,512,1024]{2,1,0:T(8,128)(2,1)}), bf16[1,4096,1024]{2,1,0:T(8,128)(2,1)}) %all-gather.5.cloned.1.call-update) | async-done | bytes 8388624 | tf_op jit(solution)/shard_map/all_gather | solution.py:92
  702.7 8.9 %fusion.5 = f32[384,1024]{1,0:T(8,128)} fusion(bf16[384,4096]{1,0:T(8,128)(2,1)} %bitcast.77, bf16[1,4096,1024]{2,1,0:T(8,128)(2,1)} %all-gather.5.cloned.1.call-done), kind=kOutput, calls=%fused_computation.8 | convolution fusion | flops 3221225472 | bytes 13107200 | tf_op jit(solution)/shard_map/dot_general | solution.py:90
  711.6 7.9 %subtract_convert_fusion = bf16[1,4096,1024]{2,1,0:T(8,128)(2,1)} fusion(bf16[1,4096,1024]{2,1,0:T(8,128)(2,1)} %param.19, f32[1024]{0:T(1024)S(1)} %get-tuple-element.43, f32[4096]{0:T(1024)S(1)} %bitcast.82), kind=kLoop, calls=%fused_computation.5 | loop fusion | flops 16777216 | bytes 16797696 | tf_op jit(solution)/shard_map/convert_element_type | solution.py:103
  721.4 3.3 reduce-scatter.5.cloned.1.call-done
  (82 shorter events, 51.2 us)
Async XLA Ops:
  7.2 179.6 %copy-start.7 = (u32[32]{0:T(128)S(1)}, u32[32]{0:T(128)}, u32[]{:S(2)}) copy-start(u32[32]{0:T(128)} %constant.111) | copy-start | bytes 388
  7.2 11.4 %copy-start.3 = (bf16[1,512,1024]{2,1,0:T(8,128)(2,1)S(1)}, bf16[1,512,1024]{2,1,0:T(8,128)(2,1)}, u32[]{:S(2)}) copy-start(bf16[1,512,1024]{2,1,0:T(8,128)(2,1)} %param.17) | copy-start | bytes 3145732
  7.2 568.3 %all-gather.7.cloned.1.call-start = ((), (), s32[]{:S(2)}) async-start(), calls=%async_computation.5 | async-start | bytes 23592960 | tf_op jit(solution)/shard_map/all_gather | solution.py:9
  18.6 684.1 %all-gather.5.cloned.1.call-start = ((), (), s32[]{:S(2)}) async-start(), calls=%async_computation.3 | async-start | bytes 9437184 | tf_op jit(solution)/shard_map/all_gather | solution.py:92
  18.6 111.5 %collective-permute-start = (bf16[1,512,1024]{2,1,0:T(8,128)(2,1)S(1)}, bf16[1,512,1024]{2,1,0:T(8,128)(2,1)S(1)}, u32[]{:S(2)}, u32[]{:S(2)}) collective-permute-start(bf16[1,512,1024]{2,1,0:T(8,128)(2,1)S(1)} %copy-done.3), channel_id=1, source_target_pairs={{0,2},{2,4},{4,6},{6,8},{8,10},{10,12},{12,14},{14,0},{1,3},{3,5},... | collective-permute-start | bytes 3145736 | tf_op jit(solution)/shard_map/ppermute | solution.py:77
  21.6 148.6 %collective-permute-start.1 = (bf16[1,512,1024]{2,1,0:T(8,128)(2,1)S(1)}, bf16[1,512,1024]{2,1,0:T(8,128)(2,1)}, u32[]{:S(2)}, u32[]{:S(2)}) collective-permute-start(bf16[1,512,1024]{2,1,0:T(8,128)(2,1)S(1)} %copy-done.3), channel_id=1, source_target_pairs={{0,14},{2,0},{4,2},{6,4},{8,6},{10,8},{12,10},{14,12},{1,15},{3,1}... | collective-permute-start | bytes 3145736 | tf_op jit(solution)/shard_map/ppermute | solution.py:82
  130.1 56.0 %copy-start.4 = (bf16[1,512,1024]{2,1,0:T(8,128)(2,1)}, bf16[1,512,1024]{2,1,0:T(8,128)(2,1)S(1)}, u32[]{:S(2)}) copy-start(bf16[1,512,1024]{2,1,0:T(8,128)(2,1)S(1)} %collective-permute-done) | copy-start | bytes 3145732
  130.1 56.0 %collective-permute-start.2 = (bf16[1,512,1024]{2,1,0:T(8,128)(2,1)S(1)}, bf16[1,512,1024]{2,1,0:T(8,128)(2,1)}, u32[]{:S(2)}, u32[]{:S(2)}) collective-permute-start(bf16[1,512,1024]{2,1,0:T(8,128)(2,1)S(1)} %collective-permute-done), channel_id=1, source_target_pairs={{0,2},{2,4},{4,6},{6,8},{8,10},{10,12},{12,14},{14,0},{1,3},{3,5},... | collective-permute-start | bytes 3145736 | tf_op jit(solution)/shard_map/ppermute | solution.py:77
  170.2 131.3 %collective-permute-start.3 = (bf16[1,512,1024]{2,1,0:T(8,128)(2,1)}, bf16[1,512,1024]{2,1,0:T(8,128)(2,1)S(1)}, u32[]{:S(2)}, u32[]{:S(2)}) collective-permute-start(bf16[1,512,1024]{2,1,0:T(8,128)(2,1)} %collective-permute-done.1), channel_id=1, source_target_pairs={{0,14},{2,0},{4,2},{6,4},{8,6},{10,8},{12,10},{14,12},{1,15},{3,1}... | collective-permute-start | bytes 3145736 | tf_op jit(solution)/shard_map/ppermute | solution.py:82
  186.1 117.7 %collective-permute-start.4 = (bf16[1,512,1024]{2,1,0:T(8,128)(2,1)}, bf16[1,512,1024]{2,1,0:T(8,128)(2,1)S(1)}, u32[]{:S(2)}, u32[]{:S(2)}) collective-permute-start(bf16[1,512,1024]{2,1,0:T(8,128)(2,1)} %collective-permute-done.2), channel_id=1, source_target_pairs={{0,2},{2,4},{4,6},{6,8},{8,10},{10,12},{12,14},{14,0},{1,3},{3,5},... | collective-permute-start | bytes 3145736 | tf_op jit(solution)/shard_map/ppermute | solution.py:77
  188.3 531.2 %reduce-scatter.3.cloned.1.call-start = ((), (), s32[]{:S(2)}) async-start(), calls=%async_computation.2 | async-start | bytes 2359296 | tf_op jit(solution)/shard_map/reduce_scatter | solution.py:96
  295.0 5.5 copy-start.5
  301.6 91.3 %collective-permute-start.5 = (bf16[1,512,1024]{2,1,0:T(8,128)(2,1)S(1)}, bf16[1,512,1024]{2,1,0:T(8,128)(2,1)S(1)}, u32[]{:S(2)}, u32[]{:S(2)}) collective-permute-start(bf16[1,512,1024]{2,1,0:T(8,128)(2,1)S(1)} %collective-permute-done.3), channel_id=1, source_target_pairs={{0,14},{2,0},{4,2},{6,4},{8,6},{10,8},{12,10},{14,12},{1,15},{3,1}... | collective-permute-start | bytes 3145736 | tf_op jit(solution)/shard_map/ppermute | solution.py:82
  303.8 90.1 %collective-permute-start.6 = (bf16[1,512,1024]{2,1,0:T(8,128)(2,1)S(1)}, bf16[1,512,1024]{2,1,0:T(8,128)(2,1)S(1)}, u32[]{:S(2)}, u32[]{:S(2)}) collective-permute-start(bf16[1,512,1024]{2,1,0:T(8,128)(2,1)S(1)} %collective-permute-done.4), channel_id=1, source_target_pairs={{0,2},{2,4},{4,6},{6,8},{8,10},{10,12},{12,14},{14,0},{1,3},{3,5},... | collective-permute-start | bytes 3145736 | tf_op jit(solution)/shard_map/ppermute | solution.py:77
  575.5 13.9 %slice-start = ((f32[640,2,4096]{2,1,0:T(2,128)}), f32[80,2,4096]{2,1,0:T(2,128)S(1)}, s32[]{:S(2)}) async-start(f32[640,2,4096]{2,1,0:T(2,128)} %all-gather.7.cloned.1.call-done), calls=%async_computation.6 | async-start | bytes 5242880 | tf_op jit(solution)/shard_map/slice | solution.py:10
  623.6 1.5 copy-start.1
  625.1 6.4 copy-start
  630.4 1.1 copy-start.2
  637.9 8.2 %copy-start.6 = (f32[4096]{0:T(1024)S(1)}, f32[4096]{0:T(1024)}, u32[]{:S(2)}) copy-start(f32[4096]{0:T(1024)} %param.16) | copy-start | bytes 49156
  654.2 70.5 %reduce-scatter.5.cloned.1.call-start = ((), (), s32[]{:S(2)}) async-start(), calls=%async_computation.4 | async-start | bytes 2359296 | tf_op jit(solution)/shard_map/reduce_scatter | solution.py:97
Sparse Core Ops, SparseCore 0:
  18.7 556.7 all-gather.6
  577.7 124.9 all-gather.4
  704.9 7.2 reduce-scatter.2
  714.4 10.2 reduce-scatter.4
